TPU v7x, 128 devices: a whole 4x4x4 slice. The times are simulated.
128 devices in a mesh: slab: 16 (over y, x), grp: 8 (over z, core).
Axes of the slice: x: 4, y: 4, z: 4, core: 2. Of those that a mesh axis runs over, the one named last changes fastest.
Arguments:
- initial: float32 [32, 64, 32, 256], P('grp', 'slab'), may hold values from 0 to 1
- target: float32 [32, 64, 32, 256], P('grp', 'slab'), may hold values from 0 to 0.6
- birth_step: int32 [64, 32, 256], P('slab'), may hold values from 0 to 4, as said below
- classes: int32 [32], P('grp'), may hold values from 0 to 3
- mobility: float32 [4, 4], replicated, may hold values from 0.2 to 2
Outputs:
- final_state: float32 [32, 64, 32, 256], P('grp', 'slab')
- initial_grad: float32 [32, 64, 32, 256], P('grp', 'slab')
- mobility_grad: float32 [4, 4], replicated
Inputs may be any that keep to these rules, and one draw needn't show every extreme that they name: A voxel takes part in step n when birth_step <= n; the value 4 means that it never takes part in the window; exactly one voxel has the value 0.
All inputs are finite; a program needn't handle non-finite values.
Results may differ from a plain program's by a relative error of at most 0.0001.
Values sent between devices are 32-bit elements; how exact they have to be, the bound alone decides.
No kernel may reach another device: no remote copies, remote signals or barrier semaphores. Data moves between devices by JAX's collectives and lax.ppermute only.
A program may use at most 64 MiB of HBM per device.

v0:
```python
import jax
import jax.numpy as jnp
from jax import lax
from jax.sharding import PartitionSpec as P

STEPS = 4
coupling = 0.3
stiffness = 1.0
time_step = 0.06


def extended_2(cells, sides, width):
    for axis, dim in sides:
        count = lax.axis_size(axis)
        ends = count - 1
        head = lax.slice_in_dim(cells, 0, width, axis=dim)
        tail = lax.slice_in_dim(cells, cells.shape[dim] - width, cells.shape[dim], axis=dim)
        cells = jnp.concatenate(
            [
                lax.ppermute(tail, axis, [(i, (i + 1) % count) for i in range(ends)]),
                cells,
                lax.ppermute(head, axis, [((i + 1) % count, i) for i in range(ends)]),
            ],
            axis=dim,
        )
    return cells


def laplace_local(extended):
    padded = jnp.pad(extended, ((0, 0), (0, 0), (1, 1), (1, 1)))
    centre = padded[:, 1:-1, 1:-1, 1:-1]
    return (
        padded[:, 2:, 1:-1, 1:-1]
        + padded[:, :-2, 1:-1, 1:-1]
        + padded[:, 1:-1, 2:, 1:-1]
        + padded[:, 1:-1, :-2, 1:-1]
        + padded[:, 1:-1, 1:-1, 2:]
        + padded[:, 1:-1, 1:-1, :-2]
        - 6.0 * centre
    )


def advance_local(fields, pair_rates, member, active):
    squared = fields * fields
    partial_sums = jnp.einsum("pk,pxzy->kxzy", member, squared, precision=lax.Precision.HIGHEST)
    class_sums = lax.psum(partial_sums, "grp")
    summed = jnp.sum(class_sums, axis=0)
    inverse = 1.0 / (1.0 + summed)
    driving = jnp.einsum("pk,kxzy->pxzy", pair_rates, class_sums, precision=lax.Precision.HIGHEST)
    rates = driving * inverse[None]
    extended = extended_2(fields, (("slab", 1),), 1)
    potential = (
        -fields
        + fields * squared
        + 2.0 * coupling * fields * (summed[None] - squared)
        - stiffness * laplace_local(extended)
    )
    weighted = active[None] * rates
    numerator, raw_denominator = lax.psum(
        (jnp.sum(weighted * potential, axis=(1, 2, 3)), jnp.sum(weighted, axis=(1, 2, 3))), "slab"
    )
    lagrange = numerator / jnp.maximum(raw_denominator, 1.0)
    updated = fields - time_step * weighted * (potential - lagrange[:, None, None, None])
    return (updated, potential, class_sums, numerator, raw_denominator)


def retreat(
    state_adj_next,
    fields,
    potential,
    class_sums,
    numerator,
    raw_denominator,
    member,
    pair_rates,
    active,
):
    squared = fields * fields
    summed = jnp.sum(class_sums, axis=0)
    inverse = 1.0 / (1.0 + summed)
    driving = jnp.einsum("pk,kxzy->pxzy", pair_rates, class_sums, precision=lax.Precision.HIGHEST)
    rates = driving * inverse[None]
    weighted = active[None] * rates
    denominator = jnp.maximum(raw_denominator, 1.0)
    lagrange = numerator / denominator
    scaled = time_step * active[None] * state_adj_next
    first_part = scaled * rates
    lagrange_adj = lax.psum(jnp.sum(first_part, axis=(1, 2, 3)), "slab")
    numer_adj = lagrange_adj / denominator
    potential_adj = weighted * numer_adj[:, None, None, None] - first_part
    extended = extended_2(potential_adj, (("slab", 1),), 1)
    curvature = laplace_local(extended)
    denom_adj = jnp.where(
        raw_denominator > 1.0, -lagrange_adj * numerator / (denominator * denominator), 0.0
    )
    rate_adj = -scaled * (potential - lagrange[:, None, None, None]) + active[None] * (
        numer_adj[:, None, None, None] * potential + denom_adj[:, None, None, None]
    )
    drive_adj = rate_adj * inverse[None]
    state_adj = (
        state_adj_next
        + potential_adj
        * (
            -1.0
            + 3.0 * squared
            + 2.0 * coupling * (summed[None] - squared)
            - 4.0 * coupling * squared
        )
        - stiffness * curvature
    )
    weighted_sums = jnp.einsum(
        "pk,pxzy->kxzy", pair_rates, drive_adj, precision=lax.Precision.HIGHEST
    )
    shared_sum = jnp.sum(
        2.0 * coupling * potential_adj * fields - (inverse * inverse)[None] * rate_adj * driving,
        axis=0,
    )
    weighted_sums, shared_sum = lax.psum((weighted_sums, shared_sum), "grp")
    class_adj = weighted_sums + shared_sum[None]
    state_adj = state_adj + 2.0 * fields * jnp.einsum(
        "pk,kxzy->pxzy", member, class_adj, precision=lax.Precision.HIGHEST
    )
    products = jnp.einsum("pxzy,kxzy->pk", drive_adj, class_sums, precision=lax.Precision.HIGHEST)
    mobility_term = jnp.dot(member.T, products, precision=lax.Precision.HIGHEST)
    return (state_adj, mobility_term)


def on_device(initial, target, birth_step, classes, mobility):
    classes_count = mobility.shape[0]
    member = (classes[:, None] == jnp.arange(classes_count, dtype=jnp.int32)[None, :]).astype(
        jnp.float32
    )
    pair_rates = jnp.dot(member, mobility, precision=lax.Precision.HIGHEST)
    fields = initial
    stored = []
    for step_index in range(STEPS):
        active = (birth_step <= step_index).astype(jnp.float32)
        updated, potential, class_sums, numerator, raw_denominator = advance_local(
            fields, pair_rates, member, active
        )
        stored.append((fields, potential, class_sums, numerator, raw_denominator, active))
        fields = updated
    state_adj = fields - target
    mobility_acc = jnp.zeros((classes_count, classes_count), jnp.float32)
    for step_index in range(STEPS - 1, -1, -1):
        saved_fields, potential, class_sums, numerator, raw_denominator, active = stored[step_index]
        state_adj, mobility_term = retreat(
            state_adj,
            saved_fields,
            potential,
            class_sums,
            numerator,
            raw_denominator,
            member,
            pair_rates,
            active,
        )
        mobility_acc = mobility_acc + mobility_term
    mobility_total = lax.psum(mobility_acc, ("slab", "grp"))
    scale = time_step * (initial.shape[1] * lax.axis_size("slab")) * initial.shape[2]
    return (fields, state_adj, mobility_total / scale)


def solution(mesh):
    return jax.shard_map(
        on_device,
        mesh=mesh,
        in_specs=(
            P("grp", "slab", None, None),
            P("grp", "slab", None, None),
            P("slab", None, None),
            P("grp"),
            P(),
        ),
        out_specs=(P("grp", "slab", None, None), P("grp", "slab", None, None), P()),
        check_vma=False,
    )
```

profile of v0, /device:TPU:0, one launch (start us, length us, event | category | flops | bytes accessed | tf_op | source)
XLA Modules:
  0.0 990.1 jit_solution(4415834130746513272)
XLA Ops:
  20.0 60.5 %all-reduce.25.cloned.1.call-done = f32[4,4,32,256]{3,0,2,1:T(4,128)} async-done(((f32[4,4,32,256]{3,0,2,1:T(4,128)}), f32[4,4,32,256]{3,0,2,1:T(4,128)}) %all-reduce.25.cloned.1.call-update) | async-done | bytes 524304 | tf_op jit(solution)/shard_map/psum | solution.py:46
  85.7 40.3 %all-reduce.11 = (f32[4]{0:T(128)S(1)}, f32[4]{0:T(128)S(1)}) all-reduce(f32[4]{0:T(128)S(1)} %get-tuple-element.13, f32[4]{0:T(128)S(1)} %get-tuple-element.12), channel_id=1, replica_groups=mesh['slab'=16,'grp'=8] {'slab'}, use_global_device_ids=true, to_apply=%region_3.4 | all-reduce | flops 8 | bytes 64 | tf_op jit(solution)/shard_map/psum | solution.py:59
  138.2 52.1 %all-reduce.27.cloned.1.call-done = f32[4,4,32,256]{3,0,2,1:T(4,128)} async-done(((f32[4,4,32,256]{3,0,2,1:T(4,128)}), f32[4,4,32,256]{3,0,2,1:T(4,128)}) %all-reduce.27.cloned.1.call-update) | async-done | bytes 524304 | tf_op jit(solution)/shard_map/psum | solution.py:46
  196.5 40.3 %all-reduce.10 = (f32[4]{0:T(128)S(1)}, f32[4]{0:T(128)S(1)}) all-reduce(f32[4]{0:T(128)S(1)} %get-tuple-element.11, f32[4]{0:T(128)S(1)} %get-tuple-element.10), channel_id=1, replica_groups=mesh['slab'=16,'grp'=8] {'slab'}, use_global_device_ids=true, to_apply=%region_9.10 | all-reduce | flops 8 | bytes 64 | tf_op jit(solution)/shard_map/psum | solution.py:59
  247.7 52.0 %all-reduce.29.cloned.1.call-done = f32[4,4,32,256]{3,0,2,1:T(4,128)} async-done(((f32[4,4,32,256]{3,0,2,1:T(4,128)}), f32[4,4,32,256]{3,0,2,1:T(4,128)}) %all-reduce.29.cloned.1.call-update) | async-done | bytes 524304 | tf_op jit(solution)/shard_map/psum | solution.py:46
  301.8 4.6 fusion.136
  306.4 40.4 %all-reduce.9 = (f32[4]{0:T(128)S(1)}, f32[4]{0:T(128)S(1)}) all-reduce(f32[4]{0:T(128)} %get-tuple-element.9, f32[4]{0:T(128)} %get-tuple-element.8), channel_id=1, replica_groups=mesh['slab'=16,'grp'=8] {'slab'}, use_global_device_ids=true, to_apply=%region_15.16 | all-reduce | flops 8 | bytes 64 | tf_op jit(solution)/shard_map/psum | solution.py:59
  359.5 51.8 %all-reduce.31.cloned.1.call-done = f32[4,4,32,256]{3,0,2,1:T(4,128)} async-done(((f32[4,4,32,256]{3,0,2,1:T(4,128)}), f32[4,4,32,256]{3,0,2,1:T(4,128)}) %all-reduce.31.cloned.1.call-update) | async-done | bytes 524304 | tf_op jit(solution)/shard_map/psum | solution.py:46
  413.4 5.4 fusion.137
  418.8 40.4 %all-reduce.8 = (f32[4]{0:T(128)S(1)}, f32[4]{0:T(128)S(1)}) all-reduce(f32[4]{0:T(128)} %get-tuple-element.7, f32[4]{0:T(128)} %get-tuple-element.6), channel_id=1, replica_groups=mesh['slab'=16,'grp'=8] {'slab'}, use_global_device_ids=true, to_apply=%region_21.22 | all-reduce | flops 8 | bytes 64 | tf_op jit(solution)/shard_map/psum | solution.py:59
  462.4 35.5 %psum.187 = f32[4]{0:T(128)S(1)} all-reduce(f32[4]{0:T(128)S(1)} %get-tuple-element.48), channel_id=1, replica_groups=mesh['slab'=16,'grp'=8] {'slab'}, use_global_device_ids=true, to_apply=%region_25.26 | all-reduce | flops 4 | bytes 32 | tf_op jit(solution)/shard_map/psum | solution.py:88
  501.9 4.5 collective-permute-start.9
  518.2 50.4 %all-reduce.39.cloned.1.call-done = (f32[4,4,32,256]{3,0,2,1:T(4,128)}, f32[4,32,256]{2,1,0:T(8,128)}) async-done(((f32[4,4,32,256]{3,0,2,1:T(4,128)}, f32[4,32,256]{2,1,0:T(8,128)}), (f32[4,4,32,256]{3,0,2,1:T(4,128)}, f32[4,32,256]{2,1,0:T(8,128)})) %all-reduce.39.cloned.1.call-update) | async-done | bytes 655376 | tf_op jit(solution)/shard_map/psum | solution.py:118
  568.6 6.0 fusion.127
  574.6 40.4 %psum.190 = f32[4]{0:T(128)S(1)} all-reduce(f32[4]{0:T(128)} %get-tuple-element.99), channel_id=1, replica_groups=mesh['slab'=16,'grp'=8] {'slab'}, use_global_device_ids=true, to_apply=%region_30.31 | all-reduce | flops 4 | bytes 32 | tf_op jit(solution)/shard_map/psum | solution.py:88
  631.7 51.4 %all-reduce.37.cloned.1.call-done = (f32[4,4,32,256]{3,0,2,1:T(4,128)}, f32[4,32,256]{2,1,0:T(8,128)}) async-done(((f32[4,4,32,256]{3,0,2,1:T(4,128)}, f32[4,32,256]{2,1,0:T(8,128)}), (f32[4,4,32,256]{3,0,2,1:T(4,128)}, f32[4,32,256]{2,1,0:T(8,128)})) %all-reduce.37.cloned.1.call-update) | async-done | bytes 655376 | tf_op jit(solution)/shard_map/psum | solution.py:118
  683.1 5.8 fusion.128
  688.9 40.8 %psum.193 = f32[4]{0:T(128)S(1)} all-reduce(f32[4]{0:T(128)} %get-tuple-element.101), channel_id=1, replica_groups=mesh['slab'=16,'grp'=8] {'slab'}, use_global_device_ids=true, to_apply=%region_35.36 | all-reduce | flops 4 | bytes 32 | tf_op jit(solution)/shard_map/psum | solution.py:88
  744.0 52.3 %all-reduce.35.cloned.1.call-done = (f32[4,4,32,256]{3,0,2,1:T(4,128)}, f32[4,32,256]{2,1,0:T(8,128)}) async-done(((f32[4,4,32,256]{3,0,2,1:T(4,128)}, f32[4,32,256]{2,1,0:T(8,128)}), (f32[4,4,32,256]{3,0,2,1:T(4,128)}, f32[4,32,256]{2,1,0:T(8,128)})) %all-reduce.35.cloned.1.call-update) | async-done | bytes 655376 | tf_op jit(solution)/shard_map/psum | solution.py:118
  796.3 5.8 fusion.129
  802.1 40.4 %psum.196 = f32[4]{0:T(128)S(1)} all-reduce(f32[4]{0:T(128)} %get-tuple-element.103), channel_id=1, replica_groups=mesh['slab'=16,'grp'=8] {'slab'}, use_global_device_ids=true, to_apply=%region_40.41 | all-reduce | flops 4 | bytes 32 | tf_op jit(solution)/shard_map/psum | solution.py:88
  851.1 62.5 %psum.199 = f32[4,4]{1,0:T(4,128)S(1)} all-reduce(f32[4,4]{1,0:T(4,128)S(1)} %convolution_add_fusion), channel_id=1, replica_groups=mesh['slab'=16,'grp'=8] {'slab','grp'}, use_global_device_ids=true, to_apply=%region_44.45 | all-reduce | flops 16 | bytes 128 | tf_op jit(solution)/shard_map/psum | solution.py:159
  917.6 4.4 collective-permute-done.14
  922.6 56.6 %all-reduce.33.cloned.1.call-done = (f32[4,4,32,256]{3,0,2,1:T(4,128)}, f32[4,32,256]{2,1,0:T(8,128)}) async-done(((f32[4,4,32,256]{3,0,2,1:T(4,128)}, f32[4,32,256]{2,1,0:T(8,128)}), (f32[4,4,32,256]{3,0,2,1:T(4,128)}, f32[4,32,256]{2,1,0:T(8,128)})) %all-reduce.33.cloned.1.call-update) | async-done | bytes 655376 | tf_op jit(solution)/shard_map/psum | solution.py:118
  (217 shorter events, 130.4 us)
Async XLA Ops:
  7.2 73.3 %all-reduce.25.cloned.1.call-start = ((), (), s32[]{:S(2)}) async-start(), calls=%async_computation | async-start | bytes 1048576 | tf_op jit(solution)/shard_map/psum | solution.py:46
  8.7 10.6 %collective-permute-start.1 = (f32[4,1,32,256]{3,0,2,1:T(4,128)S(1)}, f32[4,1,32,256]{3,0,2,1:T(4,128)S(1)}, u32[]{:S(2)}, u32[]{:S(2)}) collective-permute-start(f32[4,1,32,256]{3,0,2,1:T(4,128)S(1)} %get-tuple-element.71), channel_id=1, source_target_pairs={{0,8},{8,16},{16,24},{24,32},{32,40},{40,48},{48,56},{56,64},{64,7... | collective-permute-start | bytes 393224 | tf_op jit(solution)/shard_map/ppermute | solution.py:20
  12.4 7.0 collective-permute-start
  15.5 174.8 %all-reduce.27.cloned.1.call-start = ((), (), s32[]{:S(2)}) async-start(), calls=%async_computation.1 | async-start | bytes 1048576 | tf_op jit(solution)/shard_map/psum | solution.py:46
  128.3 4.3 collective-permute-start.3
  129.6 6.9 collective-permute-start.2
  132.6 167.1 %all-reduce.29.cloned.1.call-start = ((), (), s32[]{:S(2)}) async-start(), calls=%async_computation.2 | async-start | bytes 1048576 | tf_op jit(solution)/shard_map/psum | solution.py:46
  237.8 4.5 collective-permute-start.5
  239.1 6.9 collective-permute-start.4
  242.0 169.3 %all-reduce.31.cloned.1.call-start = ((), (), s32[]{:S(2)}) async-start(), calls=%async_computation.3 | async-start | bytes 1048576 | tf_op jit(solution)/shard_map/psum | solution.py:46
  349.4 4.3 collective-permute-start.7
  350.7 7.1 collective-permute-start.6
  353.6 215.0 %all-reduce.39.cloned.1.call-start = ((), (), s32[]{:S(2)}) async-start(), calls=%async_computation.7 | async-start | bytes 1310720 | tf_op jit(solution)/shard_map/psum | solution.py:118
  501.9 13.6 %collective-permute-start.9 = (f32[4,1,32,256]{3,0,2,1:T(4,128)}, f32[4,1,32,256]{3,0,2,1:T(4,128)}, u32[]{:S(2)}, u32[]{:S(2)}) collective-permute-start(f32[4,1,32,256]{3,0,2,1:T(4,128)} %get-tuple-element.63), channel_id=1, source_target_pairs={{0,8},{8,16},{16,24},{24,32},{32,40},{40,48},{48,56},{56,64},{64,7... | collective-permute-start | bytes 393224 | tf_op jit(solution)/shard_map/ppermute | solution.py:20
  506.4 9.0 collective-permute-start.8
  510.7 172.4 %all-reduce.37.cloned.1.call-start = ((), (), s32[]{:S(2)}) async-start(), calls=%async_computation.6 | async-start | bytes 1310720 | tf_op jit(solution)/shard_map/psum | solution.py:118
  619.5 9.5 collective-permute-start.11
  621.4 7.5 collective-permute-start.10
  624.8 171.5 %all-reduce.35.cloned.1.call-start = ((), (), s32[]{:S(2)}) async-start(), calls=%async_computation.5 | async-start | bytes 1310720 | tf_op jit(solution)/shard_map/psum | solution.py:118
  733.2 9.0 collective-permute-start.13
  734.7 7.6 collective-permute-start.12
  738.0 241.2 %all-reduce.33.cloned.1.call-start = ((), (), s32[]{:S(2)}) async-start(), calls=%async_computation.4 | async-start | bytes 1310720 | tf_op jit(solution)/shard_map/psum | solution.py:118
  913.7 3.9 collective-permute-start.15
  915.0 7.0 collective-permute-start.14
  (51 other events, 1478.6 us)
Sparse Core Ops, SparseCore 0:
  15.7 64.7 all-reduce.24
  132.7 57.5 all-reduce.26
  242.1 57.5 all-reduce.28
  353.7 57.5 all-reduce.30
  510.8 57.7 all-reduce.38
  624.9 58.1 all-reduce.36
  738.1 58.1 all-reduce.34
  916.5 62.6 all-reduce.32
where the time goes:
time: 999 us; the launch traced here: 990 us
  waiting for transfers between devices  444 us (44%)
  blocking collectives  381 us (38%)
  matrix products  68.3 us (7%)
  other arithmetic  46.8 us (5%)
  starting transfers between devices  27.8 us (3%)
  between operations  15 us (2%)
    psum x4, waiting for transfers between devices, advance_local(): class_sums = lax.psum(partial_sums, 'grp')  216 us
    psum x4, waiting for transfers between devices, retreat(): weighted_sums, shared_sum = lax.psum((weighted_sums, shared_sum), 'grp')  211 us
    psum x4, blocking collectives, advance_local(): lax.psum((jnp.sum(weighted * potential, axis=(1, 2, 3)), jnp.sum(weighted...  162 us
    psum x4, blocking collectives, retreat(): lagrange_adj = lax.psum(jnp.sum(first_part, axis=(1, 2, 3)), 'slab')  157 us
    psum x1, blocking collectives, on_device(): mobility_total = lax.psum(mobility_acc, ('slab', 'grp'))  62.5 us
    dot_general x4, matrix products, retreat(): jnp.einsum('pk,kxzy->pxzy', member, class_adj, precision=lax.Precision.HI...  20.6 us
  transfers between devices with their start and end apart: 24, of which 13 were waited for; matrix products, arithmetic and copies ran while one was open for 4% of the time, Pallas kernels for 0%

commit v1 on v0

--- a/solution.py
+++ b/solution.py
@@ -156,7 +156,8 @@
             active,
         )
         mobility_acc = mobility_acc + mobility_term
-    mobility_total = lax.psum(mobility_acc, ("slab", "grp"))
+    inner = lax.psum(mobility_acc, "grp")
+    mobility_total = lax.psum(inner, "slab")
     scale = time_step * (initial.shape[1] * lax.axis_size("slab")) * initial.shape[2]
     return (fields, state_adj, mobility_total / scale)
 

time: 999 us -> 984 us (0.985)
  blocking collectives: 381 us -> 367 us
    psum x1 -> x2, blocking collectives: 62.5 us -> 47.9 us  [the longest x1 35.4 us: on_device(): mobility_total = lax.psum(inner, 'slab')]
  transfers between devices with their start and end apart: 24 -> 24, of which waited for: 13 -> 14; matrix products, arithmetic and copies ran while one was open for 4% -> 5% of each run, Pallas kernels for 0% -> 0%
where the time goes in v1:
time: 984 us; the launch traced here: 975 us
  waiting for transfers between devices  439 us (45%)
  blocking collectives  367 us (37%)
  matrix products  70.1 us (7%)
  other arithmetic  45.5 us (5%)
  starting transfers between devices  30.4 us (3%)
  between operations  15 us (2%)
    psum x4, waiting for transfers between devices, advance_local(): class_sums = lax.psum(partial_sums, 'grp')  215 us
    psum x4, waiting for transfers between devices, retreat(): weighted_sums, shared_sum = lax.psum((weighted_sums, shared_sum), 'grp')  206 us
    psum x4, blocking collectives, advance_local(): lax.psum((jnp.sum(weighted * potential, axis=(1, 2, 3)), jnp.sum(weighted...  162 us
    psum x4, blocking collectives, retreat(): lagrange_adj = lax.psum(jnp.sum(first_part, axis=(1, 2, 3)), 'slab')  157 us
    psum x1, blocking collectives, on_device(): mobility_total = lax.psum(inner, 'slab')  35.4 us
    dot_general x4, matrix products, retreat(): jnp.einsum('pk,kxzy->pxzy', member, class_adj, precision=lax.Precision.HI...  21 us
  transfers between devices with their start and end apart: 24, of which 14 were waited for; matrix products, arithmetic and copies ran while one was open for 5% of the time, Pallas kernels for 0%

profile of v1, /device:TPU:0, one launch (start us, length us, event | category | flops | bytes accessed | tf_op | source)
XLA Modules:
  0.0 974.7 jit_solution(15163687642971807748)
XLA Ops:
  21.0 59.5 %all-reduce.25.cloned.1.call-done = f32[4,4,32,256]{3,0,2,1:T(4,128)} async-done(((f32[4,4,32,256]{3,0,2,1:T(4,128)}), f32[4,4,32,256]{3,0,2,1:T(4,128)}) %all-reduce.25.cloned.1.call-update) | async-done | bytes 524304 | tf_op jit(solution)/shard_map/psum | solution.py:46
  86.8 40.3 %all-reduce.11 = (f32[4]{0:T(128)S(1)}, f32[4]{0:T(128)S(1)}) all-reduce(f32[4]{0:T(128)S(1)} %get-tuple-element.13, f32[4]{0:T(128)S(1)} %get-tuple-element.12), channel_id=1, replica_groups=mesh['slab'=16,'grp'=8] {'slab'}, use_global_device_ids=true, to_apply=%region_3.4 | all-reduce | flops 8 | bytes 64 | tf_op jit(solution)/shard_map/psum | solution.py:59
  138.3 52.0 %all-reduce.27.cloned.1.call-done = f32[4,4,32,256]{3,0,2,1:T(4,128)} async-done(((f32[4,4,32,256]{3,0,2,1:T(4,128)}), f32[4,4,32,256]{3,0,2,1:T(4,128)}) %all-reduce.27.cloned.1.call-update) | async-done | bytes 524304 | tf_op jit(solution)/shard_map/psum | solution.py:46
  196.6 40.3 %all-reduce.10 = (f32[4]{0:T(128)S(1)}, f32[4]{0:T(128)S(1)}) all-reduce(f32[4]{0:T(128)S(1)} %get-tuple-element.11, f32[4]{0:T(128)S(1)} %get-tuple-element.10), channel_id=1, replica_groups=mesh['slab'=16,'grp'=8] {'slab'}, use_global_device_ids=true, to_apply=%region_9.10 | all-reduce | flops 8 | bytes 64 | tf_op jit(solution)/shard_map/psum | solution.py:59
  247.8 52.0 %all-reduce.29.cloned.1.call-done = f32[4,4,32,256]{3,0,2,1:T(4,128)} async-done(((f32[4,4,32,256]{3,0,2,1:T(4,128)}), f32[4,4,32,256]{3,0,2,1:T(4,128)}) %all-reduce.29.cloned.1.call-update) | async-done | bytes 524304 | tf_op jit(solution)/shard_map/psum | solution.py:46
  301.9 4.7 fusion.136
  306.7 40.4 %all-reduce.9 = (f32[4]{0:T(128)S(1)}, f32[4]{0:T(128)S(1)}) all-reduce(f32[4]{0:T(128)} %get-tuple-element.9, f32[4]{0:T(128)} %get-tuple-element.8), channel_id=1, replica_groups=mesh['slab'=16,'grp'=8] {'slab'}, use_global_device_ids=true, to_apply=%region_15.16 | all-reduce | flops 8 | bytes 64 | tf_op jit(solution)/shard_map/psum | solution.py:59
  359.8 51.8 %all-reduce.31.cloned.1.call-done = f32[4,4,32,256]{3,0,2,1:T(4,128)} async-done(((f32[4,4,32,256]{3,0,2,1:T(4,128)}), f32[4,4,32,256]{3,0,2,1:T(4,128)}) %all-reduce.31.cloned.1.call-update) | async-done | bytes 524304 | tf_op jit(solution)/shard_map/psum | solution.py:46
  413.6 5.5 fusion.137
  419.2 40.4 %all-reduce.8 = (f32[4]{0:T(128)S(1)}, f32[4]{0:T(128)S(1)}) all-reduce(f32[4]{0:T(128)} %get-tuple-element.7, f32[4]{0:T(128)} %get-tuple-element.6), channel_id=1, replica_groups=mesh['slab'=16,'grp'=8] {'slab'}, use_global_device_ids=true, to_apply=%region_21.22 | all-reduce | flops 8 | bytes 64 | tf_op jit(solution)/shard_map/psum | solution.py:59
  462.8 35.5 %psum.194 = f32[4]{0:T(128)S(1)} all-reduce(f32[4]{0:T(128)S(1)} %get-tuple-element.48), channel_id=1, replica_groups=mesh['slab'=16,'grp'=8] {'slab'}, use_global_device_ids=true, to_apply=%region_25.26 | all-reduce | flops 4 | bytes 32 | tf_op jit(solution)/shard_map/psum | solution.py:88
  502.3 4.5 collective-permute-start.9
  518.6 50.4 %all-reduce.39.cloned.1.call-done = (f32[4,4,32,256]{3,0,2,1:T(4,128)}, f32[4,32,256]{2,1,0:T(8,128)}) async-done(((f32[4,4,32,256]{3,0,2,1:T(4,128)}, f32[4,32,256]{2,1,0:T(8,128)}), (f32[4,4,32,256]{3,0,2,1:T(4,128)}, f32[4,32,256]{2,1,0:T(8,128)})) %all-reduce.39.cloned.1.call-update) | async-done | bytes 655376 | tf_op jit(solution)/shard_map/psum | solution.py:118
  569.0 6.2 fusion.127
  575.2 40.4 %psum.197 = f32[4]{0:T(128)S(1)} all-reduce(f32[4]{0:T(128)} %get-tuple-element.99), channel_id=1, replica_groups=mesh['slab'=16,'grp'=8] {'slab'}, use_global_device_ids=true, to_apply=%region_30.31 | all-reduce | flops 4 | bytes 32 | tf_op jit(solution)/shard_map/psum | solution.py:88
  632.2 51.4 %all-reduce.37.cloned.1.call-done = (f32[4,4,32,256]{3,0,2,1:T(4,128)}, f32[4,32,256]{2,1,0:T(8,128)}) async-done(((f32[4,4,32,256]{3,0,2,1:T(4,128)}, f32[4,32,256]{2,1,0:T(8,128)}), (f32[4,4,32,256]{3,0,2,1:T(4,128)}, f32[4,32,256]{2,1,0:T(8,128)})) %all-reduce.37.cloned.1.call-update) | async-done | bytes 655376 | tf_op jit(solution)/shard_map/psum | solution.py:118
  683.6 5.9 fusion.128
  689.5 40.8 %psum.200 = f32[4]{0:T(128)S(1)} all-reduce(f32[4]{0:T(128)} %get-tuple-element.101), channel_id=1, replica_groups=mesh['slab'=16,'grp'=8] {'slab'}, use_global_device_ids=true, to_apply=%region_35.36 | all-reduce | flops 4 | bytes 32 | tf_op jit(solution)/shard_map/psum | solution.py:88
  745.2 52.4 %all-reduce.35.cloned.1.call-done = (f32[4,4,32,256]{3,0,2,1:T(4,128)}, f32[4,32,256]{2,1,0:T(8,128)}) async-done(((f32[4,4,32,256]{3,0,2,1:T(4,128)}, f32[4,32,256]{2,1,0:T(8,128)}), (f32[4,4,32,256]{3,0,2,1:T(4,128)}, f32[4,32,256]{2,1,0:T(8,128)})) %all-reduce.35.cloned.1.call-update) | async-done | bytes 655376 | tf_op jit(solution)/shard_map/psum | solution.py:118
  797.6 5.9 fusion.129
  803.5 40.4 %psum.203 = f32[4]{0:T(128)S(1)} all-reduce(f32[4]{0:T(128)} %get-tuple-element.103), channel_id=1, replica_groups=mesh['slab'=16,'grp'=8] {'slab'}, use_global_device_ids=true, to_apply=%region_40.41 | all-reduce | flops 4 | bytes 32 | tf_op jit(solution)/shard_map/psum | solution.py:88
  850.4 12.4 %psum.206 = f32[4,4]{1,0:T(4,128)S(1)} all-reduce(f32[4,4]{1,0:T(4,128)S(1)} %convolution_add_fusion), channel_id=1, replica_groups=mesh['slab'=16,'grp'=8] {'grp'}, use_global_device_ids=true, to_apply=%region_44.45 | all-reduce | flops 16 | bytes 128 | tf_op jit(solution)/shard_map/psum | solution.py:159
  864.9 35.4 %psum.207 = f32[4,4]{1,0:T(4,128)S(1)} all-reduce(f32[4,4]{1,0:T(4,128)S(1)} %psum.206), channel_id=1, replica_groups=mesh['slab'=16,'grp'=8] {'slab'}, use_global_device_ids=true, to_apply=%region_45.46 | all-reduce | flops 16 | bytes 128 | tf_op jit(solution)/shard_map/psum | solution.py:160
  911.8 51.9 %all-reduce.33.cloned.1.call-done = (f32[4,4,32,256]{3,0,2,1:T(4,128)}, f32[4,32,256]{2,1,0:T(8,128)}) async-done(((f32[4,4,32,256]{3,0,2,1:T(4,128)}, f32[4,32,256]{2,1,0:T(8,128)}), (f32[4,4,32,256]{3,0,2,1:T(4,128)}, f32[4,32,256]{2,1,0:T(8,128)})) %all-reduce.33.cloned.1.call-update) | async-done | bytes 655376 | tf_op jit(solution)/shard_map/psum | solution.py:118
  (216 shorter events, 138.9 us)
Async XLA Ops:
  7.2 73.3 %all-reduce.25.cloned.1.call-start = ((), (), s32[]{:S(2)}) async-start(), calls=%async_computation | async-start | bytes 1048576 | tf_op jit(solution)/shard_map/psum | solution.py:46
  8.7 9.4 collective-permute-start.1
  12.4 6.9 collective-permute-start
  15.5 174.8 %all-reduce.27.cloned.1.call-start = ((), (), s32[]{:S(2)}) async-start(), calls=%async_computation.1 | async-start | bytes 1048576 | tf_op jit(solution)/shard_map/psum | solution.py:46
  128.4 4.3 collective-permute-start.3
  129.7 6.9 collective-permute-start.2
  132.6 167.2 %all-reduce.29.cloned.1.call-start = ((), (), s32[]{:S(2)}) async-start(), calls=%async_computation.2 | async-start | bytes 1048576 | tf_op jit(solution)/shard_map/psum | solution.py:46
  237.9 4.5 collective-permute-start.5
  239.2 6.9 collective-permute-start.4
  242.2 169.4 %all-reduce.31.cloned.1.call-start = ((), (), s32[]{:S(2)}) async-start(), calls=%async_computation.3 | async-start | bytes 1048576 | tf_op jit(solution)/shard_map/psum | solution.py:46
  349.7 4.3 collective-permute-start.7
  351.0 7.1 collective-permute-start.6
  353.9 215.1 %all-reduce.39.cloned.1.call-start = ((), (), s32[]{:S(2)}) async-start(), calls=%async_computation.7 | async-start | bytes 1310720 | tf_op jit(solution)/shard_map/psum | solution.py:118
  502.3 13.6 %collective-permute-start.9 = (f32[4,1,32,256]{3,0,2,1:T(4,128)}, f32[4,1,32,256]{3,0,2,1:T(4,128)}, u32[]{:S(2)}, u32[]{:S(2)}) collective-permute-start(f32[4,1,32,256]{3,0,2,1:T(4,128)} %get-tuple-element.63), channel_id=1, source_target_pairs={{0,8},{8,16},{16,24},{24,32},{32,40},{40,48},{48,56},{56,64},{64,7... | collective-permute-start | bytes 393224 | tf_op jit(solution)/shard_map/ppermute | solution.py:20
  506.8 9.0 collective-permute-start.8
  511.1 172.5 %all-reduce.37.cloned.1.call-start = ((), (), s32[]{:S(2)}) async-start(), calls=%async_computation.6 | async-start | bytes 1310720 | tf_op jit(solution)/shard_map/psum | solution.py:118
  620.0 9.5 collective-permute-start.11
  621.9 7.5 collective-permute-start.10
  625.3 172.3 %all-reduce.35.cloned.1.call-start = ((), (), s32[]{:S(2)}) async-start(), calls=%async_computation.5 | async-start | bytes 1310720 | tf_op jit(solution)/shard_map/psum | solution.py:118
  734.5 8.9 collective-permute-start.13
  735.8 7.6 collective-permute-start.12
  739.2 224.5 %all-reduce.33.cloned.1.call-start = ((), (), s32[]{:S(2)}) async-start(), calls=%async_computation.4 | async-start | bytes 1310720 | tf_op jit(solution)/shard_map/psum | solution.py:118
  900.4 6.4 collective-permute-start.15
  904.3 6.9 collective-permute-start.14
  (50 other events, 1680.5 us)
Sparse Core Ops, SparseCore 0:
  15.7 64.7 all-reduce.24
  132.7 57.5 all-reduce.26
  242.3 57.5 all-reduce.28
  354.0 57.5 all-reduce.30
  511.2 57.7 all-reduce.38
  625.4 58.1 all-reduce.36
  739.3 58.1 all-reduce.34
  905.9 57.7 all-reduce.32
